TPU v7x, 512 devices: a whole 4x8x8 slice. The times are simulated.
512 devices in a mesh: lat: 32 (over x, z), lev: 16 (over y, core).
Axes of the slice: x: 4, y: 8, z: 8, core: 2. Of those that a mesh axis runs over, the one named last changes fastest.
Arguments:
- fields: float32 [2, 128, 64, 3072], P(None, 'lat', 'lev'), may hold values from -6 to 6
- courant: bfloat16 [2, 128, 64, 3072], P(None, 'lat', 'lev'), may hold values from -0.3984375 to 0.3984375
- cutoffs: int32 [128], replicated, may hold values from 1 to 1536, as said below
- surface: float32 [128, 3072], P('lat'), may hold values from -6 to 6
- remap_weights: float32 [64, 64], replicated, may hold values from -0.25 to 0.75
Outputs:
- remapped: float32 [2, 128, 64, 3072], P(None, 'lat', None, 'lev')
- geopotential: float32 [128, 64, 3072], P('lat', None, 'lev')
Inputs may be any that keep to these rules, and one draw needn't show every extreme that they name: cutoffs[j] is 1536 except on the first and the last 16 latitudes, where it lies between 1 and 127; it equals 127 on some latitude among the first 16.
All inputs are finite; a program needn't handle non-finite values.
Results may differ from a plain program's by a relative error of at most 0.0003.
Values may be sent and summed in bfloat16 or wider, within the bound.
A program may use at most 64 MiB of HBM per device.

v0:
```python
import math
import jax
import jax.numpy as jnp
from jax import lax
from jax.sharding import PartitionSpec as P

KMAX = 128


def with_halo(shard, sides, width):
    for axis, dim in sides:
        size, length = (lax.axis_size(axis), shard.shape[dim])
        up = [(i, (i + 1) % size) for i in range(size - 1)]
        down = [(j, i) for i, j in up]
        last = lax.slice_in_dim(shard, length - width, length, axis=dim)
        leading = lax.slice_in_dim(shard, 0, width, axis=dim)
        before = lax.ppermute(last, axis, up)
        after = lax.ppermute(leading, axis, down)
        shard = jnp.concatenate([before, shard, after], axis=dim)
    return shard


def entering(part, axis, combine, identity):
    count = lax.axis_size(axis)
    place = lax.axis_index(axis)
    ahead = count - 1 - place
    gathered = lax.all_gather(part, axis)
    state = jnp.zeros_like(part) + jnp.asarray(identity, part.dtype)

    def one(lap, state):
        source = count - 1 - lap
        return combine(state, lax.dynamic_index_in_dim(gathered, source, 0, False))

    return lax.fori_loop(0, ahead, one, state)


def lon_part(values, east_wind):
    interface = (
        7.0 * (values + jnp.roll(values, -1, -1))
        - (jnp.roll(values, 1, -1) + jnp.roll(values, -2, -1))
    ) / 12.0
    face_wind = 0.5 * (east_wind + jnp.roll(east_wind, -1, -1))
    flux_faces = face_wind * interface
    return flux_faces - jnp.roll(flux_faces, 1, -1)


def lat_part(padded, north_wind):
    row_count = padded.shape[1] - 4
    interface = (
        7.0 * (padded[:, 1 : row_count + 2] + padded[:, 2 : row_count + 3])
        - (padded[:, 0 : row_count + 1] + padded[:, 3 : row_count + 4])
    ) / 12.0
    face_wind = 0.5 * (north_wind[0 : row_count + 1] + north_wind[1 : row_count + 2])
    flux_faces = face_wind * interface
    return flux_faces[:, 1:] - flux_faces[:, :-1]


def advance(padded, east_wind, north_wind):
    middle = padded[:, 2:-2]
    return middle - lon_part(middle, east_wind) - lat_part(padded, north_wind)


def spectral_tables(length, wave_count):
    wave_numbers = jnp.arange(wave_count, dtype=jnp.int32)
    points = jnp.arange(length, dtype=jnp.int32)
    phase = points[:, None] * wave_numbers[None, :] % length
    angle = phase.astype(jnp.float32) * (2.0 * math.pi / length)
    return (jnp.cos(angle), jnp.sin(angle))


def polar_filter(values, cutoff_rows, cosine_table, sine_table):
    length = values.shape[-1]
    wave_count = cosine_table.shape[1]
    flagged = cutoff_rows < length // 2

    def smooth(inputs):
        real_part = jnp.einsum(
            "frln,nk->frlk", inputs, cosine_table, precision=lax.Precision.HIGHEST
        )
        imag_part = jnp.einsum("frln,nk->frlk", inputs, sine_table, precision=lax.Precision.HIGHEST)
        wave_numbers = jnp.arange(wave_count, dtype=jnp.int32)
        doubled = jnp.where(wave_numbers == 0, 1.0, 2.0).astype(jnp.float32)
        weight = (
            jnp.where(wave_numbers[None, :] <= cutoff_rows[:, None], doubled[None, :], 0.0) / length
        )
        weight = weight[None, :, None, :]
        lowpass = jnp.einsum(
            "frlk,nk->frln", real_part * weight, cosine_table, precision=lax.Precision.HIGHEST
        )
        lowpass = lowpass + jnp.einsum(
            "frlk,nk->frln", imag_part * weight, sine_table, precision=lax.Precision.HIGHEST
        )
        return jnp.where(flagged[None, :, None, None], lowpass, inputs)

    return lax.cond(jnp.any(flagged), smooth, lambda inputs: inputs, values)


def upward_matrix(count):
    levels = jnp.arange(count, dtype=jnp.int32)
    deeper = (levels[None, :] > levels[:, None]).astype(jnp.float32)
    same_level = (levels[None, :] == levels[:, None]).astype(jnp.float32)
    return deeper + 0.5 * same_level


def shards(fields, courant, cutoffs, surface, remap_weights):
    band_rows = fields.shape[1]
    length = fields.shape[-1]
    nyquist = length // 2
    first_row = lax.axis_index("lat") * band_rows
    padded_cut = jnp.pad(cutoffs, 2, constant_values=nyquist)
    own_cut = lax.dynamic_slice_in_dim(padded_cut, first_row + 2, band_rows)
    cosine_table, sine_table = spectral_tables(length, KMAX)
    rim_depth = 1
    winds_rimmed = with_halo(courant, (("lat", 1),), rim_depth).astype(jnp.float32)
    east_wind = winds_rimmed[0, 1:-1]
    north_wind = winds_rimmed[1]
    transported = fields
    for repeat in range(2):
        padded = with_halo(transported, (("lat", 1),), 2)
        transported = polar_filter(
            advance(padded, east_wind, north_wind), own_cut, cosine_table, sine_table
        )
    level_count = remap_weights.shape[0]
    geo_scale = level_count ** (-0.5)
    heat_rows = transported[1]
    own_total = jnp.sum(heat_rows, axis=1)
    deeper = entering(
        own_total, "lev", lambda earlier, later: earlier + later, jnp.zeros_like(own_total)
    )
    within = jnp.einsum(
        "kl,jln->jkn", upward_matrix(heat_rows.shape[1]), heat_rows, precision=lax.Precision.HIGHEST
    )
    geo_levels = surface[:, None, :] + geo_scale * (deeper[:, None, :] + within)
    packed = jnp.concatenate([transported, geo_levels[None]], axis=0)
    columns = lax.all_to_all(packed, "lev", split_axis=3, concat_axis=2, tiled=True)
    column_columns = columns[:2]
    remapped = jnp.einsum(
        "pk,fjkn->fjpn", remap_weights, column_columns, precision=lax.Precision.HIGHEST
    )
    geo_columns = columns[2:3]
    geopotential = geo_columns[0]
    return (remapped, geopotential)


def solution(mesh):
    return jax.shard_map(
        shards,
        mesh=mesh,
        in_specs=(
            P(None, "lat", "lev", None),
            P(None, "lat", "lev", None),
            P(),
            P("lat", None),
            P(),
        ),
        out_specs=(P(None, "lat", None, "lev"), P("lat", None, "lev")),
        check_vma=False,
    )
```

profile of v0, /device:TPU:1, one launch (start us, length us, event | category | flops | bytes accessed | tf_op | source)
XLA Modules:
  0.0 197.7 jit_solution(3813942538770517226)
XLA Ops:
  0.6 0.0 copy-start
  0.6 0.0 copy-start.3
  0.7 0.9 fusion.80
  1.6 4.8 %collective-permute-start = (bf16[2,1,4,3072]{3,2,1,0:T(4,128)(2,1)S(1)}, bf16[2,1,4,3072]{3,2,1,0:T(4,128)(2,1)S(1)}, u32[]{:S(2)}, u32[]{:S(2)}) collective-permute-start(bf16[2,1,4,3072]{3,2,1,0:T(4,128)(2,1)S(1)} %get-tuple-element.130), channel_id=1, source_target_pairs={{0,16},{16,32},{32,48},{48,64},{64,80},{80,96},{96,112},{112,128},... | collective-permute-start | bytes 147464 | tf_op jit(solution)/shard_map/ppermute | solution.py:17
  6.4 1.3 collective-permute-start.1
  7.7 1.8 fusion.79
  9.5 5.3 %collective-permute-start.2 = (f32[2,2,4,3072]{3,2,1,0:T(4,128)}, f32[2,2,4,3072]{3,2,1,0:T(4,128)}, u32[]{:S(2)}, u32[]{:S(2)}) collective-permute-start(f32[2,2,4,3072]{3,2,1,0:T(4,128)} %get-tuple-element.128), channel_id=1, source_target_pairs={{0,16},{16,32},{32,48},{48,64},{64,80},{80,96},{96,112},{112,128},... | collective-permute-start | bytes 589832 | tf_op jit(solution)/shard_map/ppermute | solution.py:17
  14.8 1.3 collective-permute-start.3
  16.1 0.8 fusion.77
  16.9 1.0 fusion.78
  17.9 7.2 %fusion.35 = (f32[3072,128]{1,0:T(8,128)S(1)}, f32[3072,128]{1,0:T(8,128)}) fusion(), kind=kLoop, calls=%fused_computation.39 | loop fusion | flops 3538944 | bytes 3145728 | tf_op jit(solution)/shard_map/sin | solution.py:68
  25.1 0.1 broadcast_compare_fusion
  25.2 0.7 fusion.73
  25.9 0.3 slice.159
  26.8 0.0 slice-start
  26.8 0.0 copy-start.4
  26.8 0.2 maximum_convert_fusion
  27.0 0.2 slice_bitcast_fusion
  27.2 0.1 fusion.59
  27.3 0.1 fusion.61
  27.4 0.9 constant_dynamic-update-slice_fusion.1
  28.4 0.4 fusion.52
  28.8 0.1 slice.201
  28.9 0.2 fusion.46
  29.1 0.3 fusion.49
  29.4 6.1 %conditional.2 = (f32[2,4,4,3072]{3,2,1,0:T(4,128)S(1)}) conditional(s32[]{:T(128)} %convert_element_type.28, f32[2,4,4,3072]{3,2,1,0:T(4,128)S(1)} %fusion.49, (pred[4]{0:T(512)(128)(4,1)S(1)}, f32[2,4,4,3072]{3,2,1,0:T(4,128)S(1)}, f32[3072,128]{1,0:T(8,128)}, s32[4]{0:T(128)S(1)}, f32[3072,128]{1,0:T(8,128)}, /*index=5*/f32[3072,128]{1,0:T(8,128)S(1)}, ...), branch_computations={%region_1.2_spmd, %region_2.3_spmd} | conditional | flops 604186368 | bytes 15014968 | solution.py:95
  29.5 0.1 select_multiply_fusion
  29.6 1.1 fusion.11
  30.7 0.2 copy-done.1
  30.9 1.1 fusion.8
  32.0 1.7 fusion.4
  33.7 1.8 fusion
  35.5 0.1 fusion.74
  35.6 0.3 slice.215
  35.9 0.3 fusion.75
  36.2 4.0 %collective-permute-start.4 = (f32[2,2,4,3072]{3,2,1,0:T(4,128)S(1)}, f32[2,2,4,3072]{3,2,1,0:T(4,128)S(1)}, u32[]{:S(2)}, u32[]{:S(2)}) collective-permute-start(f32[2,2,4,3072]{3,2,1,0:T(4,128)S(1)} %get-tuple-element.119), channel_id=1, source_target_pairs={{0,16},{16,32},{32,48},{48,64},{64,80},{80,96},{96,112},{112,128},... | collective-permute-start | bytes 589832 | tf_op jit(solution)/shard_map/ppermute | solution.py:17
  40.2 1.3 collective-permute-start.5
  41.5 0.4 fusion.56
  41.9 0.1 slice.217
  41.9 0.8 collective-permute-done.4
  42.8 5.6 %collective-permute-done.5 = f32[2,2,4,3072]{3,2,1,0:T(4,128)S(1)} collective-permute-done((f32[2,2,4,3072]{3,2,1,0:T(4,128)S(1)}, f32[2,2,4,3072]{3,2,1,0:T(4,128)S(1)}, u32[]{:S(2)}, u32[]{:S(2)}) %collective-permute-start.5) | collective-permute-done | bytes 196640 | tf_op jit(solution)/shard_map/ppermute | solution.py:18
  48.4 0.2 fusion.42
  48.6 1.0 fusion.48
  49.7 9.6 %conditional.3 = (f32[2,4,4,3072]{3,2,1,0:T(4,128)}) conditional(s32[]{:T(128)} %convert_element_type.28, f32[2,4,4,3072]{3,2,1,0:T(4,128)} %fusion.48, (pred[4]{0:T(512)(128)(4,1)S(1)}, f32[2,4,4,3072]{3,2,1,0:T(4,128)}, f32[3072,128]{1,0:T(8,128)}, s32[4]{0:T(128)S(1)}, f32[3072,128]{1,0:T(8,128)}, /*index=5*/f32[3072,128]{1,0:T(8,128)S(1)}, ...), branch_computations={%region_3.4_spmd, %region_4.5_spmd} | conditional | flops 604186368 | bytes 15014968 | solution.py:95
  49.7 0.1 select_multiply_fusion.1
  49.8 2.2 %fusion.25 = f32[2,4,4,128]{3,2,1,0:T(4,128)S(1)} fusion(f32[2,4,4,3072]{3,2,1,0:T(4,128)} %get-tuple-element.89, f32[3072,128]{1,0:T(8,128)S(1)} %get-tuple-element.94, f32[4,128]{1,0:T(4,128)S(1)} %select_multiply_fusion.1), kind=kOutput, calls=%fused_computation.24 | convolution fusion | flops 150999040 | bytes 1984512 | tf_op jit(solution)/shard_map/cond/branch_1_fun/frln,nk->frlk/dot_general | solution.py:80
  52.0 2.1 %fusion.22 = f32[2,4,4,128]{3,2,1,0:T(4,128)S(1)} fusion(f32[2,4,4,3072]{3,2,1,0:T(4,128)} %get-tuple-element.89, f32[3072,128]{1,0:T(8,128)S(1)} %copy-done.2, f32[4,128]{1,0:T(4,128)S(1)} %select_multiply_fusion.1), kind=kOutput, calls=%fused_computation.23 | convolution fusion | flops 150999040 | bytes 1984512 | tf_op jit(solution)/shard_map/cond/branch_1_fun/frln,nk->frlk/dot_general | solution.py:77
  54.1 1.7 fusion.18
  55.8 3.5 %fusion.14 = f32[2,4,4,3072]{3,2,1,0:T(4,128)} fusion(f32[2,4,4,3072]{3,2,1,0:T(4,128)} %get-tuple-element.89, f32[2,4,4,3072]{3,2,1,0:T(4,128)S(1)} %fusion.18, f32[2,4,4,128]{3,2,1,0:T(4,128)S(1)} %fusion.25, f32[3072,128]{1,0:T(8,128)S(1)} %get-tuple-element.94, pred[4]{0:T(512)(128)(4,1)S(1)} %get-tuple-element.88), kind=kOutput, calls=%fused_computation.15 | convolution fusion | flops 151191552 | bytes 2768900 | tf_op jit(solution)/shard_map/cond/branch_1_fun/frlk,nk->frln/dot_general | solution.py:90
  59.3 1.0 slice_reduce_fusion
  60.3 22.4 %all-gather.1 = f32[16,4,3072]{2,1,0:T(4,128)S(1)} all-gather(f32[1,4,3072]{2,1,0:T(4,128)S(1)} %bitcast.101), channel_id=2, replica_groups=mesh['lat'=32,'lev'=16] {'lev'}, dimensions={0}, use_global_device_ids=true | all-gather | bytes 835584 | tf_op jit(solution)/shard_map/all_gather | solution.py:27
  82.7 0.7 while.12
  83.5 1.4 fusion.30
  84.9 1.1 pad_maximum_fusion
  86.0 12.7 %copy.16 = f32[3,4,4,3072]{2,1,0,3:T(4,128)} copy(f32[3,4,4,3072]{3,2,1,0:T(4,128)S(1)} %pad_maximum_fusion) | data formatting | bytes 1179648 | tf_op jit(solution)/shard_map/concatenate | solution.py:134
  98.7 24.5 %reshape.111 = f32[16,1,9216]{2,1,0:T(1,128)S(1)} reshape(f32[3072,3,4,4]{3,2,1,0:T(4,128)} %bitcast.95) | data formatting | bytes 1179648
  123.2 22.8 %all_to_all.15 = f32[16,1,9216]{2,1,0:T(1,128)S(1)} all-to-all(f32[16,1,9216]{2,1,0:T(1,128)S(1)} %reshape.111), channel_id=1, replica_groups=mesh['lat'=32,'lev'=16] {'lev'}, dimensions={0} | all-to-all | bytes 1179648 | tf_op jit(solution)/shard_map/all_to_all | solution.py:135
  146.0 0.5 broadcast.173
  146.5 2.0 %reduce.1 = f32[16,9216]{1,0:T(8,128)S(1)} reduce(f32[16,1,9216]{2,1,0:T(1,128)S(1)} %all_to_all.15, f32[]{:T(128)} %broadcast.173), dimensions={1}, to_apply=%all_to_all.11.reduce_sub_computation | reduce | bytes 1179652 | tf_op jit(solution)/shard_map/all_to_all | solution.py:135
  148.6 31.6 %reshape.112 = f32[3072,3,4,4]{3,2,1,0:T(4,128)} reshape(f32[16,9216]{1,0:T(8,128)S(1)} %reduce.1) | data formatting | bytes 1179648
  180.2 15.1 %copy.17 = f32[3,4,4,16,192]{4,2,3,1,0:T(4,128)S(1)} copy(f32[3,4,4,16,192]{2,1,0,4,3:T(4,128)} %bitcast.96) | data formatting | bytes 1179648 | tf_op jit(solution)/shard_map/all_to_all | solution.py:135
  195.3 0.2 slice.196
  195.5 0.8 squeeze.19
  196.3 1.4 convolution_bitcast_fusion
  (41 shorter events, 0.5 us)
Async XLA Ops:
  0.6 195.7 %copy-start = (f32[64,64]{1,0:T(8,128)S(1)}, f32[64,64]{1,0:T(8,128)}, u32[]{:S(2)}) copy-start(f32[64,64]{1,0:T(8,128)} %param.15) | copy-start | bytes 49156
  0.6 16.3 %copy-start.3 = (f32[2,4,4,3072]{3,2,1,0:T(4,128)S(1)}, f32[2,4,4,3072]{3,2,1,0:T(4,128)}, u32[]{:S(2)}) copy-start(f32[2,4,4,3072]{3,2,1,0:T(4,128)} %param.11) | copy-start | bytes 1179652
  1.6 25.2 %collective-permute-start = (bf16[2,1,4,3072]{3,2,1,0:T(4,128)(2,1)S(1)}, bf16[2,1,4,3072]{3,2,1,0:T(4,128)(2,1)S(1)}, u32[]{:S(2)}, u32[]{:S(2)}) collective-permute-start(bf16[2,1,4,3072]{3,2,1,0:T(4,128)(2,1)S(1)} %get-tuple-element.130), channel_id=1, source_target_pairs={{0,16},{16,32},{32,48},{48,64},{64,80},{80,96},{96,112},{112,128},... | collective-permute-start | bytes 147464 | tf_op jit(solution)/shard_map/ppermute | solution.py:17
  6.4 20.4 %collective-permute-start.1 = (bf16[2,1,4,3072]{3,2,1,0:T(4,128)(2,1)S(1)}, bf16[2,1,4,3072]{3,2,1,0:T(4,128)(2,1)S(1)}, u32[]{:S(2)}, u32[]{:S(2)}) collective-permute-start(bf16[2,1,4,3072]{3,2,1,0:T(4,128)(2,1)S(1)} %get-tuple-element.131), channel_id=1, source_target_pairs={{16,0},{32,16},{48,32},{64,48},{80,64},{96,80},{112,96},{128,112},... | collective-permute-start | bytes 147464 | tf_op jit(solution)/shard_map/ppermute | solution.py:18
  9.5 17.9 %collective-permute-start.2 = (f32[2,2,4,3072]{3,2,1,0:T(4,128)}, f32[2,2,4,3072]{3,2,1,0:T(4,128)}, u32[]{:S(2)}, u32[]{:S(2)}) collective-permute-start(f32[2,2,4,3072]{3,2,1,0:T(4,128)} %get-tuple-element.128), channel_id=1, source_target_pairs={{0,16},{16,32},{32,48},{48,64},{64,80},{80,96},{96,112},{112,128},... | collective-permute-start | bytes 589832 | tf_op jit(solution)/shard_map/ppermute | solution.py:17
  14.8 14.1 %collective-permute-start.3 = (f32[2,2,4,3072]{3,2,1,0:T(4,128)}, f32[2,2,4,3072]{3,2,1,0:T(4,128)S(1)}, u32[]{:S(2)}, u32[]{:S(2)}) collective-permute-start(f32[2,2,4,3072]{3,2,1,0:T(4,128)} %get-tuple-element.129), channel_id=1, source_target_pairs={{16,0},{32,16},{48,32},{64,48},{80,64},{96,80},{112,96},{128,112},... | collective-permute-start | bytes 589832 | tf_op jit(solution)/shard_map/ppermute | solution.py:18
  17.9 7.2 %copy-start.7 = (s32[128]{0:T(128)S(1)}, s32[128]{0:T(128)}, u32[]{:S(2)}) copy-start(s32[128]{0:T(128)} %param.13) | copy-start | bytes 1540
  17.9 8.9 %copy-start.5 = (bf16[2,4,4,3072]{3,2,1,0:T(4,128)(2,1)S(1)}, bf16[2,4,4,3072]{3,2,1,0:T(4,128)(2,1)}, u32[]{:S(2)}) copy-start(bf16[2,4,4,3072]{3,2,1,0:T(4,128)(2,1)} %param.12) | copy-start | bytes 589828
  26.8 1.6 slice-start
  26.8 1.6 copy-start.4
  29.5 1.4 copy-start.1
  36.2 6.6 %collective-permute-start.4 = (f32[2,2,4,3072]{3,2,1,0:T(4,128)S(1)}, f32[2,2,4,3072]{3,2,1,0:T(4,128)S(1)}, u32[]{:S(2)}, u32[]{:S(2)}) collective-permute-start(f32[2,2,4,3072]{3,2,1,0:T(4,128)S(1)} %get-tuple-element.119), channel_id=1, source_target_pairs={{0,16},{16,32},{32,48},{48,64},{64,80},{80,96},{96,112},{112,128},... | collective-permute-start | bytes 589832 | tf_op jit(solution)/shard_map/ppermute | solution.py:17
  40.2 8.2 %collective-permute-start.5 = (f32[2,2,4,3072]{3,2,1,0:T(4,128)S(1)}, f32[2,2,4,3072]{3,2,1,0:T(4,128)S(1)}, u32[]{:S(2)}, u32[]{:S(2)}) collective-permute-start(f32[2,2,4,3072]{3,2,1,0:T(4,128)S(1)} %get-tuple-element.120), channel_id=1, source_target_pairs={{16,0},{32,16},{48,32},{64,48},{80,64},{96,80},{112,96},{128,112},... | collective-permute-start | bytes 589832 | tf_op jit(solution)/shard_map/ppermute | solution.py:18
  49.7 2.3 %copy-start.2 = (f32[3072,128]{1,0:T(8,128)S(1)}, f32[3072,128]{1,0:T(8,128)}, u32[]{:S(2)}) copy-start(f32[3072,128]{1,0:T(8,128)} %get-tuple-element.92) | copy-start | bytes 4718596 | tf_op jit(solution)/shard_map/cond
  59.3 24.2 %copy-start.6 = (f32[4,3072]{1,0:T(4,128)S(1)}, f32[4,3072]{1,0:T(4,128)}, u32[]{:S(2)}) copy-start(f32[4,3072]{1,0:T(4,128)} %param.14) | copy-start | bytes 147460
where the time goes:
time: 199 us; the launch traced here: 198 us
  local copies, waits for them, and re-layouts  92.4 us (46%)
  blocking collectives  45.2 us (23%)
  matrix products  18.1 us (9%)
  starting transfers between devices  18 us (9%)
  other arithmetic  15.6 us (8%)
  waiting for transfers between devices  6.48 us (3%)
    unnamed x15, local copies, waits for them, and re-layouts  57.1 us
    all_to_all x1, blocking collectives, shards(): lax.all_to_all(packed, 'lev', split_axis=3, concat_axis=2, tiled=True)  22.8 us
    all_gather x1, blocking collectives, entering(): gathered = lax.all_gather(part, axis)  22.4 us
    all_to_all x2, local copies, waits for them, and re-layouts, shards(): lax.all_to_all(packed, 'lev', split_axis=3, concat_axis=2, tiled=True)  15.6 us
    ppermute x3, starting transfers between devices, with_halo(): before = lax.ppermute(last, axis, up)  14.1 us
    concatenate x1, local copies, waits for them, and re-layouts, shards(): packed = jnp.concatenate([transported, geo_levels[None]], axis=0)  12.7 us
    sin x1, other arithmetic, spectral_tables(): return (jnp.cos(angle), jnp.sin(angle))  7.19 us
    ppermute x3, waiting for transfers between devices, with_halo(): after = lax.ppermute(leading, axis, down)  5.64 us
  transfers between devices with their start and end apart: 6, of which 2 were waited for; matrix products, arithmetic and copies ran while one was open for 7% of the time, Pallas kernels for 0%

commit v1 on v0

--- a/solution.py
+++ b/solution.py
@@ -132,7 +132,10 @@
     )
     geo_levels = surface[:, None, :] + geo_scale * (deeper[:, None, :] + within)
     packed = jnp.concatenate([transported, geo_levels[None]], axis=0)
-    columns = lax.all_to_all(packed, "lev", split_axis=3, concat_axis=2, tiled=True)
+    columns = jnp.concatenate(
+        lax.all_to_all(jnp.stack(jnp.split(packed, lax.axis_size("lev"), axis=3)), "lev", 0, 0),
+        axis=2,
+    )
     column_columns = columns[:2]
     remapped = jnp.einsum(
         "pk,fjkn->fjpn", remap_weights, column_columns, precision=lax.Precision.HIGHEST

time: 199 us -> 113 us (0.57)
  local copies, waits for them, and re-layouts: 92.4 us -> 8.27 us
  other arithmetic: 15.6 us -> 11.7 us
  blocking collectives: 45.2 us -> 49.1 us
    unnamed x15 -> x13, local copies, waits for them, and re-layouts: 57.1 us -> 0.97 us
    all_to_all x2 -> x0, local copies, waits for them, and re-layouts: 15.6 us -> none  [shards(): lax.all_to_all(packed, 'lev', split_axis=3, concat_axis=2, tiled=True)]
    concatenate x1 -> x0, local copies, waits for them, and re-layouts: 12.7 us -> none  [shards(): packed = jnp.concatenate([transported, geo_levels[None]], axis=0)]
    all_to_all x1, blocking collectives: 22.8 us -> 26.7 us  [shards(): lax.all_to_all(jnp.stack(jnp.split(packed, lax.axis_size('lev'), axis=3))...]
    all_to_all x1 -> x0, other arithmetic: 2.04 us -> none  [shards(): lax.all_to_all(packed, 'lev', split_axis=3, concat_axis=2, tiled=True)]
    dot_general x2, matrix products: 3.25 us -> 5.26 us  [smooth(): jnp.einsum('frln,nk->frlk', inputs, cosine_table, precision=lax.Precision...]
  transfers between devices with their start and end apart: 6 -> 6, of which waited for: 2 -> 2; matrix products, arithmetic and copies ran while one was open for 7% -> 13% of each run, Pallas kernels for 0% -> 0%
where the time goes in v1:
time: 113 us; the launch traced here: 112 us
  blocking collectives  49.1 us (43%)
  starting transfers between devices  18 us (16%)
  matrix products  16.4 us (15%)
  other arithmetic  11.7 us (10%)
  local copies, waits for them, and re-layouts  8.27 us (7%)
  waiting for transfers between devices  6.48 us (6%)
  between operations  1.75 us (2%)
    all_to_all x1, blocking collectives, shards(): lax.all_to_all(jnp.stack(jnp.split(packed, lax.axis_size('lev'), axis=3))...  26.7 us
    all_gather x1, blocking collectives, entering(): gathered = lax.all_gather(part, axis)  22.4 us
    ppermute x3, starting transfers between devices, with_halo(): before = lax.ppermute(last, axis, up)  14.1 us
    sin x1, other arithmetic, spectral_tables(): return (jnp.cos(angle), jnp.sin(angle))  7.2 us
    ppermute x3, waiting for transfers between devices, with_halo(): after = lax.ppermute(leading, axis, down)  5.64 us
    dot_general x2, matrix products, smooth(): jnp.einsum('frln,nk->frlk', inputs, cosine_table, precision=lax.Precision...  5.26 us
    ppermute x3, starting transfers between devices, with_halo(): after = lax.ppermute(leading, axis, down)  3.86 us
    dot_general x2, matrix products, smooth(): jnp.einsum('frlk,nk->frln', imag_part * weight, sine_table, precision=lax...  3.63 us
  transfers between devices with their start and end apart: 6, of which 2 were waited for; matrix products, arithmetic and copies ran while one was open for 13% of the time, Pallas kernels for 0%

profile of v1, /device:TPU:1, one launch (start us, length us, event | category | flops | bytes accessed | tf_op | source)
XLA Modules:
  0.0 112.4 jit_solution(13110372620379916036)
XLA Ops:
  0.6 0.0 copy-start
  0.6 0.0 copy-start.3
  0.7 0.9 fusion.97
  1.6 4.8 %collective-permute-start = (bf16[2,1,4,3072]{3,2,1,0:T(4,128)(2,1)S(1)}, bf16[2,1,4,3072]{3,2,1,0:T(4,128)(2,1)S(1)}, u32[]{:S(2)}, u32[]{:S(2)}) collective-permute-start(bf16[2,1,4,3072]{3,2,1,0:T(4,128)(2,1)S(1)} %get-tuple-element.130), channel_id=1, source_target_pairs={{0,16},{16,32},{32,48},{48,64},{64,80},{80,96},{96,112},{112,128},... | collective-permute-start | bytes 147464 | tf_op jit(solution)/shard_map/ppermute | solution.py:17
  6.4 1.3 %collective-permute-start.1 = (bf16[2,1,4,3072]{3,2,1,0:T(4,128)(2,1)S(1)}, bf16[2,1,4,3072]{3,2,1,0:T(4,128)(2,1)S(1)}, u32[]{:S(2)}, u32[]{:S(2)}) collective-permute-start(bf16[2,1,4,3072]{3,2,1,0:T(4,128)(2,1)S(1)} %get-tuple-element.131), channel_id=1, source_target_pairs={{16,0},{32,16},{48,32},{64,48},{80,64},{96,80},{112,96},{128,112},... | collective-permute-start | bytes 147464 | tf_op jit(solution)/shard_map/ppermute | solution.py:18
  7.7 1.8 %fusion.96 = (f32[2,2,4,3072]{3,2,1,0:T(4,128)}, f32[2,2,4,3072]{3,2,1,0:T(4,128)}) fusion(f32[2,4,4,3072]{3,2,1,0:T(4,128)} %param.11), kind=kLoop, calls=%fused_computation.178 | loop fusion | bytes 786432 | tf_op jit(solution)/shard_map/slice | solution.py:15
  9.5 5.3 %collective-permute-start.2 = (f32[2,2,4,3072]{3,2,1,0:T(4,128)}, f32[2,2,4,3072]{3,2,1,0:T(4,128)}, u32[]{:S(2)}, u32[]{:S(2)}) collective-permute-start(f32[2,2,4,3072]{3,2,1,0:T(4,128)} %get-tuple-element.128), channel_id=1, source_target_pairs={{0,16},{16,32},{32,48},{48,64},{64,80},{80,96},{96,112},{112,128},... | collective-permute-start | bytes 589832 | tf_op jit(solution)/shard_map/ppermute | solution.py:17
  14.8 1.3 %collective-permute-start.3 = (f32[2,2,4,3072]{3,2,1,0:T(4,128)}, f32[2,2,4,3072]{3,2,1,0:T(4,128)S(1)}, u32[]{:S(2)}, u32[]{:S(2)}) collective-permute-start(f32[2,2,4,3072]{3,2,1,0:T(4,128)} %get-tuple-element.129), channel_id=1, source_target_pairs={{16,0},{32,16},{48,32},{64,48},{80,64},{96,80},{112,96},{128,112},... | collective-permute-start | bytes 589832 | tf_op jit(solution)/shard_map/ppermute | solution.py:18
  16.1 2.1 %fusion.95 = (f32[2,4,4,3071]{3,2,1,0:T(4,128)S(1)}, f32[2,4,4,3071]{3,2,1,0:T(4,128)}) fusion(f32[2,4,4,3072]{3,2,1,0:T(4,128)} %param.11), kind=kLoop, calls=%fused_computation.177 | loop fusion | bytes 1572352 | tf_op jit(solution)/shard_map/jit(_roll_static)/slice | solution.py:40
  18.2 0.1 fusion.94
  18.3 7.2 %fusion.35 = (f32[3072,128]{1,0:T(8,128)S(1)}, f32[3072,128]{1,0:T(8,128)}) fusion(), kind=kLoop, calls=%fused_computation.54 | loop fusion | flops 3538944 | bytes 3145728 | tf_op jit(solution)/shard_map/sin | solution.py:68
  25.5 0.1 broadcast_compare_fusion
  25.6 0.7 fusion.90
  26.3 0.3 slice.159
  27.3 0.0 slice-start
  27.3 0.0 copy-start.4
  27.3 0.2 maximum_convert_fusion
  27.6 0.2 slice_bitcast_fusion
  27.7 0.1 fusion.59
  27.8 0.1 fusion.61
  27.9 0.9 constant_dynamic-update-slice_fusion.1
  28.9 0.4 fusion.52
  29.3 0.1 slice.201
  29.4 0.2 fusion.46
  29.7 0.3 fusion.49
  30.0 7.4 %conditional.2 = (f32[2,4,4,3072]{3,2,1,0:T(4,128)S(1)}) conditional(s32[]{:T(128)} %convert_element_type.28, f32[2,4,4,3072]{3,2,1,0:T(4,128)S(1)} %fusion.49, (pred[4]{0:T(512)(128)(4,1)S(1)}, f32[2,4,4,3072]{3,2,1,0:T(4,128)S(1)}, f32[3072,128]{1,0:T(8,128)}, s32[4]{0:T(128)S(1)}, f32[3072,128]{1,0:T(8,128)}, /*index=5*/f32[3072,128]{1,0:T(8,128)S(1)}, ...), branch_computations={%region_1.2_spmd, %region_2.3_spmd} | conditional | flops 604186368 | bytes 15014968 | solution.py:95
  30.0 0.1 select_multiply_fusion
  30.1 2.6 %fusion.8 = f32[2,4,4,128]{3,2,1,0:T(4,128)S(1)} fusion(f32[2,4,4,3072]{3,2,1,0:T(4,128)S(1)} %get-tuple-element.82, f32[3072,128]{1,0:T(8,128)} %get-tuple-element.85, f32[4,128]{1,0:T(4,128)S(1)} %select_multiply_fusion), kind=kOutput, calls=%fused_computation.9 | convolution fusion | flops 150999040 | bytes 1984512 | tf_op jit(solution)/shard_map/cond/branch_1_fun/frln,nk->frlk/dot_general | solution.py:77
  32.7 1.7 %fusion.4 = f32[2,4,4,3072]{3,2,1,0:T(4,128)S(1)} fusion(f32[2,4,4,128]{3,2,1,0:T(4,128)S(1)} %fusion.8, f32[3072,128]{1,0:T(8,128)S(1)} %copy-done.1), kind=kOutput, calls=%fused_computation.5 | convolution fusion | flops 150994944 | bytes 1982464 | tf_op jit(solution)/shard_map/cond/branch_1_fun/frlk,nk->frln/dot_general | solution.py:87
  34.4 1.1 %fusion.11 = f32[2,4,4,128]{3,2,1,0:T(4,128)S(1)} fusion(f32[2,4,4,3072]{3,2,1,0:T(4,128)S(1)} %get-tuple-element.82, f32[3072,128]{1,0:T(8,128)S(1)} %get-tuple-element.87, f32[4,128]{1,0:T(4,128)S(1)} %select_multiply_fusion), kind=kOutput, calls=%fused_computation.10 | convolution fusion | flops 150999040 | bytes 1984512 | tf_op jit(solution)/shard_map/cond/branch_1_fun/frln,nk->frlk/dot_general | solution.py:80
  35.6 1.8 %fusion = f32[2,4,4,3072]{3,2,1,0:T(4,128)S(1)} fusion(f32[2,4,4,3072]{3,2,1,0:T(4,128)S(1)} %get-tuple-element.82, f32[2,4,4,3072]{3,2,1,0:T(4,128)S(1)} %fusion.4, f32[2,4,4,128]{3,2,1,0:T(4,128)S(1)} %fusion.11, f32[3072,128]{1,0:T(8,128)S(1)} %get-tuple-element.87, pred[4]{0:T(512)(128)(4,1)S(1)} %get-tuple-element.81), kind=kOutput, calls=%fused_computation.1 | convolution fusion | flops 151191552 | bytes 2768900 | tf_op jit(solution)/shard_map/cond/branch_1_fun/frlk,nk->frln/dot_general | solution.py:90
  37.4 0.3 fusion.92
  37.6 0.3 slice.215
  37.9 0.1 fusion.91
  38.0 4.0 %collective-permute-start.4 = (f32[2,2,4,3072]{3,2,1,0:T(4,128)S(1)}, f32[2,2,4,3072]{3,2,1,0:T(4,128)S(1)}, u32[]{:S(2)}, u32[]{:S(2)}) collective-permute-start(f32[2,2,4,3072]{3,2,1,0:T(4,128)S(1)} %get-tuple-element.119), channel_id=1, source_target_pairs={{0,16},{16,32},{32,48},{48,64},{64,80},{80,96},{96,112},{112,128},... | collective-permute-start | bytes 589832 | tf_op jit(solution)/shard_map/ppermute | solution.py:17
  42.0 1.3 %collective-permute-start.5 = (f32[2,2,4,3072]{3,2,1,0:T(4,128)S(1)}, f32[2,2,4,3072]{3,2,1,0:T(4,128)S(1)}, u32[]{:S(2)}, u32[]{:S(2)}) collective-permute-start(f32[2,2,4,3072]{3,2,1,0:T(4,128)S(1)} %get-tuple-element.120), channel_id=1, source_target_pairs={{16,0},{32,16},{48,32},{64,48},{80,64},{96,80},{112,96},{128,112},... | collective-permute-start | bytes 589832 | tf_op jit(solution)/shard_map/ppermute | solution.py:18
  43.3 0.4 fusion.56
  43.7 0.1 slice.217
  43.8 0.8 collective-permute-done.4
  44.6 5.6 %collective-permute-done.5 = f32[2,2,4,3072]{3,2,1,0:T(4,128)S(1)} collective-permute-done((f32[2,2,4,3072]{3,2,1,0:T(4,128)S(1)}, f32[2,2,4,3072]{3,2,1,0:T(4,128)S(1)}, u32[]{:S(2)}, u32[]{:S(2)}) %collective-permute-start.5) | collective-permute-done | bytes 196640 | tf_op jit(solution)/shard_map/ppermute | solution.py:18
  50.3 0.2 fusion.42
  50.5 0.3 fusion.48
  50.8 7.6 %conditional.3 = (f32[2,4,4,3072]{3,2,1,0:T(4,128)S(1)}) conditional(s32[]{:T(128)} %convert_element_type.28, f32[2,4,4,3072]{3,2,1,0:T(4,128)S(1)} %fusion.48, (pred[4]{0:T(512)(128)(4,1)S(1)}, f32[2,4,4,3072]{3,2,1,0:T(4,128)S(1)}, f32[3072,128]{1,0:T(8,128)}, s32[4]{0:T(128)S(1)}, f32[3072,128]{1,0:T(8,128)}, /*index=5*/f32[3072,128]{1,0:T(8,128)S(1)}, ...), branch_computations={%region_3.4_spmd, %region_4.5_spmd} | conditional | flops 604186368 | bytes 15014968 | solution.py:95
  51.0 0.1 select_multiply_fusion.1
  51.1 2.6 %fusion.22 = f32[2,4,4,128]{3,2,1,0:T(4,128)S(1)} fusion(f32[2,4,4,3072]{3,2,1,0:T(4,128)S(1)} %get-tuple-element.89, f32[3072,128]{1,0:T(8,128)} %get-tuple-element.92, f32[4,128]{1,0:T(4,128)S(1)} %select_multiply_fusion.1), kind=kOutput, calls=%fused_computation.23 | convolution fusion | flops 150999040 | bytes 1984512 | tf_op jit(solution)/shard_map/cond/branch_1_fun/frln,nk->frlk/dot_general | solution.py:77
  53.7 1.7 %fusion.18 = f32[2,4,4,3072]{3,2,1,0:T(4,128)S(1)} fusion(f32[2,4,4,128]{3,2,1,0:T(4,128)S(1)} %fusion.22, f32[3072,128]{1,0:T(8,128)S(1)} %copy-done.2), kind=kOutput, calls=%fused_computation.19 | convolution fusion | flops 150994944 | bytes 1982464 | tf_op jit(solution)/shard_map/cond/branch_1_fun/frlk,nk->frln/dot_general | solution.py:87
  55.4 1.1 %fusion.25 = f32[2,4,4,128]{3,2,1,0:T(4,128)S(1)} fusion(f32[2,4,4,3072]{3,2,1,0:T(4,128)S(1)} %get-tuple-element.89, f32[3072,128]{1,0:T(8,128)S(1)} %get-tuple-element.94, f32[4,128]{1,0:T(4,128)S(1)} %select_multiply_fusion.1), kind=kOutput, calls=%fused_computation.24 | convolution fusion | flops 150999040 | bytes 1984512 | tf_op jit(solution)/shard_map/cond/branch_1_fun/frln,nk->frlk/dot_general | solution.py:80
  56.6 1.8 %fusion.14 = f32[2,4,4,3072]{3,2,1,0:T(4,128)S(1)} fusion(f32[2,4,4,3072]{3,2,1,0:T(4,128)S(1)} %get-tuple-element.89, f32[2,4,4,3072]{3,2,1,0:T(4,128)S(1)} %fusion.18, f32[2,4,4,128]{3,2,1,0:T(4,128)S(1)} %fusion.25, f32[3072,128]{1,0:T(8,128)S(1)} %get-tuple-element.94, pred[4]{0:T(512)(128)(4,1)S(1)} %get-tuple-element.88), kind=kOutput, calls=%fused_computation.15 | convolution fusion | flops 151191552 | bytes 2768900 | tf_op jit(solution)/shard_map/cond/branch_1_fun/frlk,nk->frln/dot_general | solution.py:90
  58.4 0.1 slice_reduce_fusion
  58.5 22.4 %all-gather.1 = f32[16,4,3072]{2,1,0:T(4,128)S(1)} all-gather(f32[1,4,3072]{2,1,0:T(4,128)S(1)} %bitcast.130), channel_id=2, replica_groups=mesh['lat'=32,'lev'=16] {'lev'}, dimensions={0}, use_global_device_ids=true | all-gather | bytes 835584 | tf_op jit(solution)/shard_map/all_gather | solution.py:27
  80.9 0.8 while.12
  81.7 0.5 fusion.30
  82.2 0.1 bitcast_dynamic-update-slice_fusion.13
  82.3 0.1 bitcast_dynamic-update-slice_fusion.11
  82.4 0.1 bitcast_dynamic-update-slice_fusion.9
  82.6 0.1 bitcast_dynamic-update-slice_fusion.7
  82.7 0.1 bitcast_dynamic-update-slice_fusion.5
  82.8 0.1 bitcast_dynamic-update-slice_fusion.3
  83.0 0.1 bitcast_dynamic-update-slice_fusion.1
  83.1 0.1 fusion.80
  83.2 26.7 %all_to_all.5 = f32[16,3,4,4,192]{4,3,2,1,0:T(4,128)S(1)} all-to-all(f32[16,3,4,4,192]{4,3,2,1,0:T(4,128)S(1)} %fusion.80), channel_id=1, replica_groups=mesh['lat'=32,'lev'=16] {'lev'}, dimensions={0} | all-to-all | bytes 1179648 | tf_op jit(solution)/shard_map/all_to_all | solution.py:136
  110.0 0.2 slice.196
  110.2 0.8 squeeze.19
  111.0 1.4 %convolution_bitcast_fusion = f32[2,4,64,192]{3,2,1,0:T(8,128)} fusion(f32[2,4,64,192]{3,2,1,0:T(8,128)S(1)} %slice.196, f32[64,64]{1,0:T(8,128)S(1)} %copy-done), kind=kOutput, calls=%fused_computation.57 | convolution fusion | flops 75497472 | bytes 802816 | tf_op jit(solution)/shard_map/pk,fjkn->fjpn/dot_general | solution.py:140
  (52 shorter events, 0.8 us)
Async XLA Ops:
  0.6 110.4 %copy-start = (f32[64,64]{1,0:T(8,128)S(1)}, f32[64,64]{1,0:T(8,128)}, u32[]{:S(2)}) copy-start(f32[64,64]{1,0:T(8,128)} %param.15) | copy-start | bytes 49156
  0.6 17.6 %copy-start.3 = (f32[2,4,4,3072]{3,2,1,0:T(4,128)S(1)}, f32[2,4,4,3072]{3,2,1,0:T(4,128)}, u32[]{:S(2)}) copy-start(f32[2,4,4,3072]{3,2,1,0:T(4,128)} %param.11) | copy-start | bytes 1179652
  1.6 25.7 %collective-permute-start = (bf16[2,1,4,3072]{3,2,1,0:T(4,128)(2,1)S(1)}, bf16[2,1,4,3072]{3,2,1,0:T(4,128)(2,1)S(1)}, u32[]{:S(2)}, u32[]{:S(2)}) collective-permute-start(bf16[2,1,4,3072]{3,2,1,0:T(4,128)(2,1)S(1)} %get-tuple-element.130), channel_id=1, source_target_pairs={{0,16},{16,32},{32,48},{48,64},{64,80},{80,96},{96,112},{112,128},... | collective-permute-start | bytes 147464 | tf_op jit(solution)/shard_map/ppermute | solution.py:17
  6.4 20.9 %collective-permute-start.1 = (bf16[2,1,4,3072]{3,2,1,0:T(4,128)(2,1)S(1)}, bf16[2,1,4,3072]{3,2,1,0:T(4,128)(2,1)S(1)}, u32[]{:S(2)}, u32[]{:S(2)}) collective-permute-start(bf16[2,1,4,3072]{3,2,1,0:T(4,128)(2,1)S(1)} %get-tuple-element.131), channel_id=1, source_target_pairs={{16,0},{32,16},{48,32},{64,48},{80,64},{96,80},{112,96},{128,112},... | collective-permute-start | bytes 147464 | tf_op jit(solution)/shard_map/ppermute | solution.py:18
  9.5 18.4 %collective-permute-start.2 = (f32[2,2,4,3072]{3,2,1,0:T(4,128)}, f32[2,2,4,3072]{3,2,1,0:T(4,128)}, u32[]{:S(2)}, u32[]{:S(2)}) collective-permute-start(f32[2,2,4,3072]{3,2,1,0:T(4,128)} %get-tuple-element.128), channel_id=1, source_target_pairs={{0,16},{16,32},{32,48},{48,64},{64,80},{80,96},{96,112},{112,128},... | collective-permute-start | bytes 589832 | tf_op jit(solution)/shard_map/ppermute | solution.py:17
  14.8 14.6 %collective-permute-start.3 = (f32[2,2,4,3072]{3,2,1,0:T(4,128)}, f32[2,2,4,3072]{3,2,1,0:T(4,128)S(1)}, u32[]{:S(2)}, u32[]{:S(2)}) collective-permute-start(f32[2,2,4,3072]{3,2,1,0:T(4,128)} %get-tuple-element.129), channel_id=1, source_target_pairs={{16,0},{32,16},{48,32},{64,48},{80,64},{96,80},{112,96},{128,112},... | collective-permute-start | bytes 589832 | tf_op jit(solution)/shard_map/ppermute | solution.py:18
  18.3 7.2 %copy-start.7 = (s32[128]{0:T(128)S(1)}, s32[128]{0:T(128)}, u32[]{:S(2)}) copy-start(s32[128]{0:T(128)} %param.13) | copy-start | bytes 1540
  18.3 9.0 %copy-start.5 = (bf16[2,4,4,3072]{3,2,1,0:T(4,128)(2,1)S(1)}, bf16[2,4,4,3072]{3,2,1,0:T(4,128)(2,1)}, u32[]{:S(2)}) copy-start(bf16[2,4,4,3072]{3,2,1,0:T(4,128)(2,1)} %param.12) | copy-start | bytes 589828
  27.3 1.6 %slice-start = ((f32[2,4,4,3072]{3,2,1,0:T(4,128)}), f32[2,4,4,2]{3,2,1,0:T(4,128)S(1)}, s32[]{:S(2)}) async-start(f32[2,4,4,3072]{3,2,1,0:T(4,128)} %param.11), calls=%async_computation.1 | async-start | bytes 32768 | tf_op jit(solution)/shard_map/jit(_roll_static)/slice | solution.py:40
  27.3 1.6 %copy-start.4 = (f32[2,4,4,3071]{3,2,1,0:T(4,128)S(1)}, f32[2,4,4,3071]{3,2,1,0:T(4,128)}, u32[]{:S(2)}) copy-start(f32[2,4,4,3071]{3,2,1,0:T(4,128)} %get-tuple-element.127) | copy-start | bytes 1179268
  30.0 2.7 %copy-start.1 = (f32[3072,128]{1,0:T(8,128)S(1)}, f32[3072,128]{1,0:T(8,128)}, u32[]{:S(2)}) copy-start(f32[3072,128]{1,0:T(8,128)} %get-tuple-element.85) | copy-start | bytes 4718596 | tf_op jit(solution)/shard_map/cond
  38.0 6.6 %collective-permute-start.4 = (f32[2,2,4,3072]{3,2,1,0:T(4,128)S(1)}, f32[2,2,4,3072]{3,2,1,0:T(4,128)S(1)}, u32[]{:S(2)}, u32[]{:S(2)}) collective-permute-start(f32[2,2,4,3072]{3,2,1,0:T(4,128)S(1)} %get-tuple-element.119), channel_id=1, source_target_pairs={{0,16},{16,32},{32,48},{48,64},{64,80},{80,96},{96,112},{112,128},... | collective-permute-start | bytes 589832 | tf_op jit(solution)/shard_map/ppermute | solution.py:17
  42.0 8.2 %collective-permute-start.5 = (f32[2,2,4,3072]{3,2,1,0:T(4,128)S(1)}, f32[2,2,4,3072]{3,2,1,0:T(4,128)S(1)}, u32[]{:S(2)}, u32[]{:S(2)}) collective-permute-start(f32[2,2,4,3072]{3,2,1,0:T(4,128)S(1)} %get-tuple-element.120), channel_id=1, source_target_pairs={{16,0},{32,16},{48,32},{64,48},{80,64},{96,80},{112,96},{128,112},... | collective-permute-start | bytes 589832 | tf_op jit(solution)/shard_map/ppermute | solution.py:18
  51.0 2.7 %copy-start.2 = (f32[3072,128]{1,0:T(8,128)S(1)}, f32[3072,128]{1,0:T(8,128)}, u32[]{:S(2)}) copy-start(f32[3072,128]{1,0:T(8,128)} %get-tuple-element.92) | copy-start | bytes 4718596 | tf_op jit(solution)/shard_map/cond
  58.4 23.3 %copy-start.6 = (f32[4,3072]{1,0:T(4,128)S(1)}, f32[4,3072]{1,0:T(4,128)}, u32[]{:S(2)}) copy-start(f32[4,3072]{1,0:T(4,128)} %param.14) | copy-start | bytes 147460
